TPU v7x, 512 devices: a whole 4x8x8 slice. The times are simulated.
512 devices in a mesh: seq: 32 (over y_hi, z, core), chan: 16 (over x, y_lo).
Axes of the slice: x: 4, y: 8 (y_hi: 2, y_lo: 4; y = y_hi * 4 + y_lo), z: 8, core: 2. Of those that a mesh axis runs over, the one named last changes fastest.
Arguments:
- values: bfloat16 [4096, 1024], P('seq', 'chan'), may hold values from -6 to 6
- gate_inner: bfloat16 [4096, 1024], P('seq', 'chan'), may hold values from -6 to 6
- gate_outer: bfloat16 [4096, 1024], P('seq', 'chan'), may hold values from -6 to 6
- filter_one: float32 [16, 4096], P('chan', 'seq'), may hold values from -0.09375 to 0.09375
- filter_two: float32 [16, 4096], P('chan', 'seq'), may hold values from -0.09375 to 0.09375
- teacher: bfloat16 [4096, 1024], P('seq', 'chan'), may hold values from -6 to 6
- w_out: bfloat16 [1024, 1024], P(None, 'chan'), may hold values from -0.1875 to 0.1875
- gene_ids: int32 [4096], P('seq'), may hold values from 0 to 25425
- cell_lengths: int32 [4], replicated, may hold values from 1 to 2048, 4096 in all
- gene_weights: float32 [25426], replicated, may hold values from 0.5 to 2
Outputs:
- grad_values: bfloat16 [4096, 1024], P('seq', 'chan')
- grad_inner: bfloat16 [4096, 1024], P('seq', 'chan')
- grad_outer: bfloat16 [4096, 1024], P('seq', 'chan')
- grad_filter_one: float32 [16, 4096], P('chan', 'seq')
- grad_filter_two: float32 [16, 4096], P('chan', 'seq')
- grad_w_out: float32 [1024, 1024], P('seq', 'chan')
Inputs may be any that keep to these rules, and one draw needn't show every extreme that they name: `cell_lengths`: the lengths sum to 4096, and the largest equals 2048.
All inputs are finite; a program needn't handle non-finite values.
Results may differ from a plain program's by a relative error of at most 0.0051.
Values may be sent and summed in bfloat16 or wider, within the bound.
A program may use at most 64 MiB of HBM per device.

v0:
```python
import jax
import jax.numpy as jnp
from jax import lax
from jax.sharding import PartitionSpec as P

TWO_PI = 6.283185307179586
PRECISE = lax.Precision.HIGHEST


def phases(left_index, right_index, modulus):
    turn_count = left_index[:, None] * right_index[None, :] % modulus
    centred = jnp.where(2 * turn_count > modulus, turn_count - modulus, turn_count)
    radians = centred.astype(jnp.float32) * (TWO_PI / modulus)
    return (jnp.cos(radians), jnp.sin(radians))


def make_tables(length, shard_count, position):
    stride = length // shard_count
    lane_index = jnp.arange(shard_count, dtype=jnp.int32)
    doubled = jnp.arange(2 * shard_count, dtype=jnp.int32)
    padded_len = 2 * shard_count * length
    offsets = jnp.arange(length, dtype=jnp.int32)
    wide_cos, wide_sin = phases(lane_index, doubled, 2 * shard_count)
    near_cos, near_sin = phases(
        position * stride + jnp.arange(stride, dtype=jnp.int32), doubled, padded_len
    )
    far_cos, far_sin = phases(offsets, 2 * position + jnp.arange(2, dtype=jnp.int32), padded_len)
    long_cos, long_sin = phases(offsets, offsets, length)
    return (wide_cos, wide_sin, near_cos, near_sin, far_cos, far_sin, long_cos, long_sin)


def spread_out(packed):
    return lax.all_to_all(packed, "seq", split_axis=0, concat_axis=1, tiled=True)


def bring_back(packed):
    return lax.all_to_all(packed, "seq", split_axis=1, concat_axis=0, tiled=True)


def halves(packed):
    half_width = packed.shape[-1] // 2
    return (packed[..., :half_width], packed[..., half_width:])


def long_transform(real_in, imag_in, table_cos, table_sin, sign):
    shape_in = real_in.shape
    stacked = jnp.concatenate(
        [real_in.reshape(shape_in[0], -1), imag_in.reshape(shape_in[0], -1)], axis=1
    )
    cos_part = jnp.dot(table_cos, stacked, precision=PRECISE)
    sin_part = jnp.dot(table_sin, stacked, precision=PRECISE)
    cos_real, cos_imag = halves(cos_part)
    sin_real, sin_imag = halves(sin_part)
    real_out = cos_real + sign * sin_imag
    imag_out = cos_imag - sign * sin_real
    return (real_out.reshape(shape_in), imag_out.reshape(shape_in))


def forward_columns(columns, tables):
    wide_cos, wide_sin, near_cos, near_sin, far_cos, far_sin, long_cos, long_sin = tables
    real_part = jnp.einsum("rnf,nk->rkf", columns, wide_cos, precision=PRECISE)
    imag_part = -jnp.einsum("rnf,nk->rkf", columns, wide_sin, precision=PRECISE)
    twist_cos = near_cos[:, :, None]
    twist_sin = near_sin[:, :, None]
    turned = jnp.concatenate(
        [
            real_part * twist_cos + imag_part * twist_sin,
            imag_part * twist_cos - real_part * twist_sin,
        ],
        axis=2,
    )
    arrived_real, arrived_imag = halves(bring_back(turned))
    return long_transform(arrived_real, arrived_imag, long_cos, long_sin, 1.0)


def inverse_columns(spectra, tables):
    wide_cos, wide_sin, near_cos, near_sin, far_cos, far_sin, long_cos, long_sin = tables
    time_real, time_imag = long_transform(spectra[0], spectra[1], long_cos, long_sin, -1.0)
    twist_cos = far_cos[:, :, None]
    twist_sin = far_sin[:, :, None]
    turned = jnp.concatenate(
        [
            time_real * twist_cos - time_imag * twist_sin,
            time_imag * twist_cos + time_real * twist_sin,
        ],
        axis=2,
    )
    arrived_real, arrived_imag = halves(spread_out(turned))
    padded_len = 2 * wide_cos.shape[0] * spectra[0].shape[0]
    summed = jnp.einsum("rkf,nk->rnf", arrived_real, wide_cos, precision=PRECISE) - jnp.einsum(
        "rkf,nk->rnf", arrived_imag, wide_sin, precision=PRECISE
    )
    return summed * (1.0 / padded_len)


def spectrum(block_data, tables):
    return forward_columns(spread_out(block_data[:, None, :]), tables)


def signal_rows(spectra, tables):
    arrived = bring_back(inverse_columns(spectra, tables))
    return arrived.reshape(arrived.shape[0], -1)


def take_range(spectra, start, stop):
    return (spectra[0][..., start:stop], spectra[1][..., start:stop])


def joined(first_pair, second_pair):
    return (
        jnp.concatenate([first_pair[0], second_pair[0]], axis=-1),
        jnp.concatenate([first_pair[1], second_pair[1]], axis=-1),
    )


def filtered(spectra, filters, conjugate):
    groups = filters[0].shape[-1]
    shape_in = spectra[0].shape
    split_shape = shape_in[:-1] + (groups, shape_in[-1] // groups)
    left_real = spectra[0].reshape(split_shape)
    left_imag = spectra[1].reshape(split_shape)
    right_real = filters[0][..., None]
    right_imag = filters[1][..., None] * (-1.0 if conjugate else 1.0)
    out_real = left_real * right_real - left_imag * right_imag
    out_imag = left_real * right_imag + left_imag * right_real
    return (out_real.reshape(shape_in), out_imag.reshape(shape_in))


def pooled(first_pair, second_pair, groups):
    shape_in = first_pair[0].shape
    split_shape = shape_in[:-1] + (groups, shape_in[-1] // groups)
    left_real = first_pair[0].reshape(split_shape)
    left_imag = first_pair[1].reshape(split_shape)
    right_real = second_pair[0].reshape(split_shape)
    right_imag = second_pair[1].reshape(split_shape)
    out_real = jnp.sum(left_real * right_real + left_imag * right_imag, axis=-1)
    out_imag = jnp.sum(left_real * right_imag - left_imag * right_real, axis=-1)
    return (out_real, out_imag)


def project(pooled_in, target, weights, w_cols):
    gathered = lax.all_gather(pooled_in, "chan", axis=1, tiled=True)
    output = jnp.dot(gathered, w_cols, preferred_element_type=jnp.float32)
    deviation = (weights[:, None] * (output - target.astype(jnp.float32))).astype(jnp.bfloat16)
    partial_w = lax.dot_general(
        gathered, deviation, (((0,), (0,)), ((), ())), preferred_element_type=jnp.float32
    )
    weight_grad = lax.psum_scatter(partial_w, "seq", scatter_dimension=0, tiled=True)
    channel_back = lax.psum_scatter(
        lax.dot_general(
            w_cols, deviation, (((1,), (1,)), ((), ())), preferred_element_type=jnp.float32
        ),
        "chan",
        scatter_dimension=0,
        tiled=True,
    )
    back_outer = channel_back.T
    return (back_outer, weight_grad)


def per_device(
    values,
    gate_inner,
    gate_outer,
    filter_one,
    filter_two,
    teacher,
    w_out,
    gene_ids,
    cell_lengths,
    gene_weights,
):
    shard_count = lax.axis_size("seq")
    position = lax.axis_index("seq")
    length = values.shape[0]
    channels = values.shape[1]
    groups = filter_one.shape[0]
    tables = make_tables(length, shard_count, position)
    token_pos = position * length + jnp.arange(length, dtype=jnp.int32)
    starts = jnp.cumsum(cell_lengths) - cell_lengths
    opening = jnp.any(token_pos[:, None] == starts[None, :], axis=1)
    weights = jnp.take(gene_weights, gene_ids, axis=0) * jnp.where(opening, 0.0, 1.0)
    stacked = jnp.concatenate([values.astype(jnp.float32), filter_one.T, filter_two.T], axis=1)
    spectra = spectrum(stacked, tables)
    spec_values = take_range(spectra, 0, channels)
    spec_one = take_range(spectra, channels, channels + groups)
    spec_two = take_range(spectra, channels + groups, channels + 2 * groups)
    first_conv = signal_rows(filtered(spec_values, spec_one, False), tables)
    spec_inner = spectrum(gate_inner * first_conv, tables)
    second_conv = signal_rows(filtered(spec_inner, spec_two, False), tables)
    pooled_in = (gate_outer * second_conv).astype(jnp.bfloat16)
    back_outer, grad_w_out = project(pooled_in, teacher, weights, w_out)
    grad_outer = (back_outer * second_conv).astype(jnp.bfloat16)
    spec_second = spectrum(back_outer * gate_outer, tables)
    merged = signal_rows(
        joined(filtered(spec_second, spec_two, True), pooled(spec_inner, spec_second, groups)),
        tables,
    )
    back_inner = merged[:, :channels]
    grad_two = merged[:, channels:]
    grad_inner = (back_inner * first_conv).astype(jnp.bfloat16)
    spec_first = spectrum(back_inner * gate_inner, tables)
    merged = signal_rows(
        joined(filtered(spec_first, spec_one, True), pooled(spec_values, spec_first, groups)),
        tables,
    )
    grad_values = merged[:, :channels].astype(jnp.bfloat16)
    grad_one = merged[:, channels:]
    return (grad_values, grad_inner, grad_outer, grad_one.T, grad_two.T, grad_w_out)


def solution(mesh):
    return jax.shard_map(
        per_device,
        mesh=mesh,
        in_specs=(
            P("seq", "chan"),
            P("seq", "chan"),
            P("seq", "chan"),
            P("chan", "seq"),
            P("chan", "seq"),
            P("seq", "chan"),
            P(None, "chan"),
            P("seq"),
            P(),
            P(),
        ),
        out_specs=(
            P("seq", "chan"),
            P("seq", "chan"),
            P("seq", "chan"),
            P("chan", "seq"),
            P("chan", "seq"),
            P("seq", "chan"),
        ),
        check_vma=False,
    )
```

profile of v0, /device:TPU:4, one launch (start us, length us, event | category | flops | bytes accessed | tf_op | source)
XLA Modules:
  0.0 558.9 jit_solution(16846920802349217116)
XLA Ops:
  10.2 16.0 %all-to-all-start = ((f32[128,1,66]{2,1,0:T(1,128)}), f32[128,1,66]{2,1,0:T(1,128)S(1)}, u32[]{:S(2)}, u32[]{:S(2)}) async-start(f32[128,1,66]{2,1,0:T(1,128)} %copy.332), calls=%async_computation | async-start | bytes 131072 | tf_op jit(solution)/shard_map/all_to_all | solution.py:33
  26.3 12.4 %all-to-all-done = f32[128,1,66]{2,1,0:T(1,128)S(1)} async-done(((f32[128,1,66]{2,1,0:T(1,128)}), f32[128,1,66]{2,1,0:T(1,128)S(1)}, u32[]{:S(2)}, u32[]{:S(2)}) %all-to-all-start) | async-done | bytes 33824 | tf_op jit(solution)/shard_map/all_to_all | solution.py:33
  44.5 14.4 %all-to-all-done.1 = f32[4,64,132]{2,0,1:T(4,128)S(1)} async-done(((f32[4,64,132]{2,0,1:T(4,128)}), f32[4,64,132]{2,0,1:T(4,128)S(1)}, u32[]{:S(2)}, u32[]{:S(2)}) %all-to-all-start.1) | async-done | bytes 135200 | tf_op jit(solution)/shard_map/all_to_all | solution.py:37
  62.3 18.0 %all_to_all.276 = f32[128,2,128]{2,1,0:T(2,128)S(1)} all-to-all(f32[128,2,128]{2,1,0:T(2,128)S(1)} %copy.341), channel_id=1, replica_groups=mesh['seq'=32,'chan'=16] {'seq'}, dimensions={0} | all-to-all | bytes 262144 | tf_op jit(solution)/shard_map/all_to_all | solution.py:33
  85.9 12.3 %all-to-all-done.3 = f32[32,1,256]{2,1,0:T(1,128)S(1)} async-done(((f32[32,1,256]{2,1,0:T(1,128)}), f32[32,1,256]{2,1,0:T(1,128)S(1)}, u32[]{:S(2)}, u32[]{:S(2)}) %all-to-all-start.3) | async-done | bytes 32800 | tf_op jit(solution)/shard_map/all_to_all | solution.py:37
  100.5 15.4 %all_to_all.277 = f32[32,1,256]{2,1,0:T(1,128)S(1)} all-to-all(f32[32,1,256]{2,1,0:T(1,128)S(1)} %reshape.510), channel_id=1, replica_groups=mesh['seq'=32,'chan'=16] {'seq'}, dimensions={0} | all-to-all | bytes 65536 | tf_op jit(solution)/shard_map/all_to_all | solution.py:33
  118.3 4.0 all-to-all-start.5
  123.4 12.1 %all-to-all-done.5 = f32[4,64,128]{2,0,1:T(4,128)S(1)} async-done(((f32[4,64,128]{2,0,1:T(4,128)}), f32[4,64,128]{2,0,1:T(4,128)S(1)}, u32[]{:S(2)}, u32[]{:S(2)}) %all-to-all-start.5) | async-done | bytes 131104 | tf_op jit(solution)/shard_map/all_to_all | solution.py:37
  139.0 4.2 all-to-all-start.6
  144.4 11.6 %all-to-all-done.6 = f32[128,2,128]{2,1,0:T(2,128)S(1)} async-done(((f32[128,2,128]{2,1,0:T(2,128)}), f32[128,2,128]{2,1,0:T(2,128)S(1)}, u32[]{:S(2)}, u32[]{:S(2)}) %all-to-all-start.6) | async-done | bytes 131104 | tf_op jit(solution)/shard_map/all_to_all | solution.py:33
  161.7 12.2 %all-to-all-done.7 = f32[32,1,256]{2,1,0:T(1,128)S(1)} async-done(((f32[32,1,256]{2,1,0:T(1,128)}), f32[32,1,256]{2,1,0:T(1,128)S(1)}, u32[]{:S(2)}, u32[]{:S(2)}) %all-to-all-start.7) | async-done | bytes 32800 | tf_op jit(solution)/shard_map/all_to_all | solution.py:37
  174.8 36.0 %all_gather.3 = bf16[128,1024]{0,1:T(8,128)(2,1)S(1)} all-gather(bf16[128,64]{0,1:T(8,128)(2,1)S(1)} %copy.361), channel_id=1, replica_groups=mesh['seq'=32,'chan'=16] {'chan'}, dimensions={1}, use_global_device_ids=true | all-gather | bytes 278528 | tf_op jit(solution)/shard_map/all_gather | solution.py:142
  212.2 71.3 %reduce-scatter.7.cloned.1.call-done = f32[64,128]{1,0:T(8,128)} async-done(((f32[1024,128]{1,0:T(8,128)}), f32[64,128]{1,0:T(8,128)}) %reduce-scatter.7.cloned.1.call-update) | async-done | bytes 32784
  285.3 22.2 %all_to_all.278 = f32[32,1,256]{2,1,0:T(1,128)S(1)} all-to-all(f32[32,1,256]{2,1,0:T(1,128)S(1)} %reshape.514), channel_id=1, replica_groups=mesh['seq'=32,'chan'=16] {'seq'}, dimensions={0} | all-to-all | bytes 65536 | tf_op jit(solution)/shard_map/all_to_all | solution.py:33
  313.9 13.1 %all-to-all-done.9 = f32[4,64,128]{2,0,1:T(4,128)S(1)} async-done(((f32[4,64,128]{2,0,1:T(4,128)}), f32[4,64,128]{2,0,1:T(4,128)S(1)}, u32[]{:S(2)}, u32[]{:S(2)}) %all-to-all-start.9) | async-done | bytes 131104 | tf_op jit(solution)/shard_map/all_to_all | solution.py:37
  330.5 17.8 %all_to_all.279 = f32[128,2,130]{2,1,0:T(2,128)S(1)} all-to-all(f32[128,2,130]{2,1,0:T(2,128)S(1)} %copy.374), channel_id=1, replica_groups=mesh['seq'=32,'chan'=16] {'seq'}, dimensions={0} | all-to-all | bytes 266240 | tf_op jit(solution)/shard_map/all_to_all | solution.py:33
  349.3 17.2 %all_to_all.280 = f32[4,32,65]{2,0,1:T(4,128)S(1)} all-to-all(f32[4,32,65]{2,0,1:T(4,128)S(1)} %copy.376), channel_id=1, replica_groups=mesh['seq'=32,'chan'=16] {'seq'}, dimensions={1} | all-to-all | bytes 66560 | tf_op jit(solution)/shard_map/all_to_all | solution.py:37
  367.4 15.3 %all_to_all.281 = f32[32,1,256]{2,1,0:T(1,128)S(1)} all-to-all(f32[32,1,256]{2,1,0:T(1,128)S(1)} %reshape.516), channel_id=1, replica_groups=mesh['seq'=32,'chan'=16] {'seq'}, dimensions={0} | all-to-all | bytes 65536 | tf_op jit(solution)/shard_map/all_to_all | solution.py:33
  385.2 4.1 all-to-all-start.13
  389.3 12.9 %all-to-all-done.13 = f32[4,64,128]{2,0,1:T(4,128)S(1)} async-done(((f32[4,64,128]{2,0,1:T(4,128)}), f32[4,64,128]{2,0,1:T(4,128)S(1)}, u32[]{:S(2)}, u32[]{:S(2)}) %all-to-all-start.13) | async-done | bytes 131104 | tf_op jit(solution)/shard_map/all_to_all | solution.py:37
  412.5 12.1 %all-to-all-done.14 = f32[128,2,130]{2,1,0:T(2,128)S(1)} async-done(((f32[128,2,130]{2,1,0:T(2,128)}), f32[128,2,130]{2,1,0:T(2,128)S(1)}, u32[]{:S(2)}, u32[]{:S(2)}) %all-to-all-start.14) | async-done | bytes 133152 | tf_op jit(solution)/shard_map/all_to_all | solution.py:33
  426.0 5.0 all-to-all-start.15
  431.7 11.8 %all-to-all-done.15 = f32[4,32,65]{2,0,1:T(4,128)S(1)} async-done(((f32[4,32,65]{2,0,1:T(4,128)}), f32[4,32,65]{2,0,1:T(4,128)S(1)}, u32[]{:S(2)}, u32[]{:S(2)}) %all-to-all-start.15) | async-done | bytes 33312 | tf_op jit(solution)/shard_map/all_to_all | solution.py:37
  444.9 106.5 %reduce-scatter.5.cloned.1.call-done = f32[32,64]{1,0:T(8,128)} async-done(((f32[1024,64]{1,0:T(8,128)}), f32[32,64]{1,0:T(8,128)}) %reduce-scatter.5.cloned.1.call-update) | async-done | bytes 8208 | tf_op jit(solution)/shard_map/reduce_scatter | solution.py:148
  (208 shorter events, 64.5 us)
Async XLA Ops:
  8.0 202.8 %copy-start = (bf16[1024,64]{0,1:T(8,128)(2,1)S(1)}, bf16[1024,64]{0,1:T(8,128)(2,1)}, u32[]{:S(2)}) copy-start(bf16[1024,64]{0,1:T(8,128)(2,1)} %param.16) | copy-start | bytes 393220
  8.8 0.7 copy-start.5
  8.8 0.7 copy-start.6
  10.2 28.5 %all-to-all-start = ((f32[128,1,66]{2,1,0:T(1,128)}), f32[128,1,66]{2,1,0:T(1,128)S(1)}, u32[]{:S(2)}, u32[]{:S(2)}) async-start(f32[128,1,66]{2,1,0:T(1,128)} %copy.332), calls=%async_computation | async-start | bytes 131072 | tf_op jit(solution)/shard_map/all_to_all | solution.py:33
  40.5 18.4 %all-to-all-start.1 = ((f32[4,64,132]{2,0,1:T(4,128)}), f32[4,64,132]{2,0,1:T(4,128)S(1)}, u32[]{:S(2)}, u32[]{:S(2)}) async-start(f32[4,64,132]{2,0,1:T(4,128)} %copy.334), calls=%async_computation.1 | async-start | bytes 524288 | tf_op jit(solution)/shard_map/all_to_all | solution.py:37
  81.8 4.0 copy-start.2
  81.8 16.4 %all-to-all-start.3 = ((f32[32,1,256]{2,1,0:T(1,128)}), f32[32,1,256]{2,1,0:T(1,128)S(1)}, u32[]{:S(2)}, u32[]{:S(2)}) async-start(f32[32,1,256]{2,1,0:T(1,128)} %reshape.508), calls=%async_computation.3 | async-start | bytes 65536 | tf_op jit(solution)/shard_map/all_to_all | solution.py:37
  118.3 4.0 copy-start.7
  118.3 17.1 %all-to-all-start.5 = ((f32[4,64,128]{2,0,1:T(4,128)}), f32[4,64,128]{2,0,1:T(4,128)S(1)}, u32[]{:S(2)}, u32[]{:S(2)}) async-start(f32[4,64,128]{2,0,1:T(4,128)} %copy.347), calls=%async_computation.5 | async-start | bytes 262144 | tf_op jit(solution)/shard_map/all_to_all | solution.py:37
  122.3 0.7 copy-start.8
  139.0 4.2 copy-start.1
  139.0 17.1 %all-to-all-start.6 = ((f32[128,2,128]{2,1,0:T(2,128)}), f32[128,2,128]{2,1,0:T(2,128)S(1)}, u32[]{:S(2)}, u32[]{:S(2)}) async-start(f32[128,2,128]{2,1,0:T(2,128)} %copy.357), calls=%async_computation.6 | async-start | bytes 262144 | tf_op jit(solution)/shard_map/all_to_all | solution.py:33
  157.5 4.0 copy-start.3
  157.5 16.3 %all-to-all-start.7 = ((f32[32,1,256]{2,1,0:T(1,128)}), f32[32,1,256]{2,1,0:T(1,128)S(1)}, u32[]{:S(2)}, u32[]{:S(2)}) async-start(f32[32,1,256]{2,1,0:T(1,128)} %reshape.512), calls=%async_computation.7 | async-start | bytes 65536 | tf_op jit(solution)/shard_map/all_to_all | solution.py:37
  161.5 122.1 %reduce-scatter.7.cloned.1.call-start = ((), (), s32[]{:S(2)}) async-start(), calls=%async_computation.19 | async-start | bytes 557056
  174.8 36.0 %copy-start.4 = (bf16[128,64]{0,1:T(8,128)(2,1)S(1)}, bf16[128,64]{0,1:T(8,128)(2,1)}, u32[]{:S(2)}) copy-start(bf16[128,64]{0,1:T(8,128)(2,1)} %param.15) | copy-start | bytes 49156
  310.0 17.0 %all-to-all-start.9 = ((f32[4,64,128]{2,0,1:T(4,128)}), f32[4,64,128]{2,0,1:T(4,128)S(1)}, u32[]{:S(2)}, u32[]{:S(2)}) async-start(f32[4,64,128]{2,0,1:T(4,128)} %copy.364), calls=%async_computation.9 | async-start | bytes 262144 | tf_op jit(solution)/shard_map/all_to_all | solution.py:37
  385.2 17.0 %all-to-all-start.13 = ((f32[4,64,128]{2,0,1:T(4,128)}), f32[4,64,128]{2,0,1:T(4,128)S(1)}, u32[]{:S(2)}, u32[]{:S(2)}) async-start(f32[4,64,128]{2,0,1:T(4,128)} %copy.379), calls=%async_computation.13 | async-start | bytes 262144 | tf_op jit(solution)/shard_map/all_to_all | solution.py:37
  406.1 18.4 %all-to-all-start.14 = ((f32[128,2,130]{2,1,0:T(2,128)}), f32[128,2,130]{2,1,0:T(2,128)S(1)}, u32[]{:S(2)}, u32[]{:S(2)}) async-start(f32[128,2,130]{2,1,0:T(2,128)} %copy.385), calls=%async_computation.14 | async-start | bytes 524288 | tf_op jit(solution)/shard_map/all_to_all | solution.py:33
  410.0 141.4 %reduce-scatter.5.cloned.1.call-start = ((), (), s32[]{:S(2)}) async-start(), calls=%async_computation.18 | async-start | bytes 540672 | tf_op jit(solution)/shard_map/reduce_scatter | solution.py:148
  426.0 17.5 %all-to-all-start.15 = ((f32[4,32,65]{2,0,1:T(4,128)}), f32[4,32,65]{2,0,1:T(4,128)S(1)}, u32[]{:S(2)}, u32[]{:S(2)}) async-start(f32[4,32,65]{2,0,1:T(4,128)} %copy.387), calls=%async_computation.15 | async-start | bytes 131072 | tf_op jit(solution)/shard_map/all_to_all | solution.py:37
Sparse Core Ops, SparseCore 0:
  212.4 71.1 reduce-scatter.6
Sparse Core Ops, SparseCore 1:
  416.3 135.0 reduce-scatter.4
where the time goes:
time: 560 us; the launch traced here: 559 us
  waiting for transfers between devices  303 us (54%)
  blocking collectives  142 us (25%)
  starting transfers between devices  52.7 us (9%)
  local copies, waits for them, and re-layouts  20.5 us (4%)
  between operations  16.6 us (3%)
  matrix products  16 us (3%)
  other arithmetic  8.36 us (1%)
    reduce_scatter x1, waiting for transfers between devices, project(): lax.psum_scatter(partial_w, 'seq', scatter_dimension=0, tiled=True)  107 us
    all_to_all x7, waiting for transfers between devices, bring_back(): lax.all_to_all(packed, 'seq', split_axis=1, concat_axis=0, tiled=True)  88.8 us
    all_to_all x5, blocking collectives, spread_out(): lax.all_to_all(packed, 'seq', split_axis=0, concat_axis=1, tiled=True)  88.7 us
    unnamed x3, waiting for transfers between devices  71.3 us
    all_to_all x3, waiting for transfers between devices, spread_out(): lax.all_to_all(packed, 'seq', split_axis=0, concat_axis=1, tiled=True)  36 us
    all_gather x1, blocking collectives, project(): gathered = lax.all_gather(pooled_in, 'chan', axis=1, tiled=True)  36 us
    all_to_all x7, starting transfers between devices, bring_back(): lax.all_to_all(packed, 'seq', split_axis=1, concat_axis=0, tiled=True)  28.6 us
    all_to_all x3, starting transfers between devices, spread_out(): lax.all_to_all(packed, 'seq', split_axis=0, concat_axis=1, tiled=True)  24 us
  transfers between devices with their start and end apart: 12, of which 12 were waited for; matrix products, arithmetic and copies ran while one was open for 1% of the time, Pallas kernels for 0%

commit v1 on v0

--- a/solution.py
+++ b/solution.py
@@ -1,3 +1,4 @@
+import functools
 import jax
 import jax.numpy as jnp
 from jax import lax
@@ -5,6 +6,17 @@
 
 TWO_PI = 6.283185307179586
 PRECISE = lax.Precision.HIGHEST
+
+
+def return_all_ratios_all(vector, lane_axis):
+    left_arr = lax.axis_size(lane_axis)
+    e_now = jnp.stack(left_arr * [vector])
+    inter = lax.all_to_all(e_now, split_axis=0, axis_name=lane_axis, concat_axis=0)
+    opened = jnp.concatenate(inter, axis=1)
+    return opened
+
+
+state_attach = functools.partial(return_all_ratios_all, lane_axis="chan")
 
 
 def phases(left_index, right_index, modulus):
@@ -139,7 +151,7 @@
 
 
 def project(pooled_in, target, weights, w_cols):
-    gathered = lax.all_gather(pooled_in, "chan", axis=1, tiled=True)
+    gathered = state_attach(pooled_in)
     output = jnp.dot(gathered, w_cols, preferred_element_type=jnp.float32)
     deviation = (weights[:, None] * (output - target.astype(jnp.float32))).astype(jnp.bfloat16)
     partial_w = lax.dot_general(

time: 560 us -> 539 us (0.963)
  the two profiles are of different devices: /device:TPU:4 before, /device:TPU:2 now
where the time goes in v1:
time: 539 us; the launch traced here: 537 us
  waiting for transfers between devices  308 us (57%)
  blocking collectives  106 us (20%)
  starting transfers between devices  60.6 us (11%)
  local copies, waits for them, and re-layouts  21.3 us (4%)
  between operations  16.6 us (3%)
  matrix products  16.1 us (3%)
  other arithmetic  8.36 us (2%)
    reduce_scatter x1, waiting for transfers between devices, project(): lax.psum_scatter(partial_w, 'seq', scatter_dimension=0, tiled=True)  103 us
    all_to_all x7, waiting for transfers between devices, bring_back(): lax.all_to_all(packed, 'seq', split_axis=1, concat_axis=0, tiled=True)  89.5 us
    all_to_all x5, blocking collectives, spread_out(): lax.all_to_all(packed, 'seq', split_axis=0, concat_axis=1, tiled=True)  88.6 us
    unnamed x3, waiting for transfers between devices  72.7 us
    all_to_all x3, waiting for transfers between devices, spread_out(): lax.all_to_all(packed, 'seq', split_axis=0, concat_axis=1, tiled=True)  36.4 us
    all_to_all x7, starting transfers between devices, bring_back(): lax.all_to_all(packed, 'seq', split_axis=1, concat_axis=0, tiled=True)  28.6 us
    all_to_all x3, starting transfers between devices, spread_out(): lax.all_to_all(packed, 'seq', split_axis=0, concat_axis=1, tiled=True)  23.9 us
    all_to_all x1, blocking collectives, bring_back(): lax.all_to_all(packed, 'seq', split_axis=1, concat_axis=0, tiled=True)  17.5 us
  transfers between devices with their start and end apart: 13, of which 13 were waited for; matrix products, arithmetic and copies ran while one was open for 1% of the time, Pallas kernels for 0%

profile of v1, /device:TPU:2, one launch (start us, length us, event | category | flops | bytes accessed | tf_op | source)
XLA Modules:
  0.0 537.4 jit_solution(7701910242564440795)
XLA Ops:
  10.2 16.0 %all-to-all-start = ((f32[128,1,66]{2,1,0:T(1,128)}), f32[128,1,66]{2,1,0:T(1,128)S(1)}, u32[]{:S(2)}, u32[]{:S(2)}) async-start(f32[128,1,66]{2,1,0:T(1,128)} %copy.334), calls=%async_computation | async-start | bytes 131072 | tf_op jit(solution)/shard_map/all_to_all | solution.py:45
  26.3 12.4 %all-to-all-done = f32[128,1,66]{2,1,0:T(1,128)S(1)} async-done(((f32[128,1,66]{2,1,0:T(1,128)}), f32[128,1,66]{2,1,0:T(1,128)S(1)}, u32[]{:S(2)}, u32[]{:S(2)}) %all-to-all-start) | async-done | bytes 33824 | tf_op jit(solution)/shard_map/all_to_all | solution.py:45
  44.5 14.4 %all-to-all-done.1 = f32[4,64,132]{2,0,1:T(4,128)S(1)} async-done(((f32[4,64,132]{2,0,1:T(4,128)}), f32[4,64,132]{2,0,1:T(4,128)S(1)}, u32[]{:S(2)}, u32[]{:S(2)}) %all-to-all-start.1) | async-done | bytes 135200 | tf_op jit(solution)/shard_map/all_to_all | solution.py:49
  62.3 18.0 %all_to_all.281 = f32[128,2,128]{2,1,0:T(2,128)S(1)} all-to-all(f32[128,2,128]{2,1,0:T(2,128)S(1)} %copy.343), channel_id=1, replica_groups=mesh['seq'=32,'chan'=16] {'seq'}, dimensions={0} | all-to-all | bytes 262144 | tf_op jit(solution)/shard_map/all_to_all | solution.py:45
  85.9 12.3 %all-to-all-done.3 = f32[32,1,256]{2,1,0:T(1,128)S(1)} async-done(((f32[32,1,256]{2,1,0:T(1,128)}), f32[32,1,256]{2,1,0:T(1,128)S(1)}, u32[]{:S(2)}, u32[]{:S(2)}) %all-to-all-start.3) | async-done | bytes 32800 | tf_op jit(solution)/shard_map/all_to_all | solution.py:49
  100.4 15.4 %all_to_all.282 = f32[32,1,256]{2,1,0:T(1,128)S(1)} all-to-all(f32[32,1,256]{2,1,0:T(1,128)S(1)} %reshape.520), channel_id=1, replica_groups=mesh['seq'=32,'chan'=16] {'seq'}, dimensions={0} | all-to-all | bytes 65536 | tf_op jit(solution)/shard_map/all_to_all | solution.py:45
  122.4 12.9 %all-to-all-done.5 = f32[4,64,128]{2,0,1:T(4,128)S(1)} async-done(((f32[4,64,128]{2,0,1:T(4,128)}), f32[4,64,128]{2,0,1:T(4,128)S(1)}, u32[]{:S(2)}, u32[]{:S(2)}) %all-to-all-start.5) | async-done | bytes 131104 | tf_op jit(solution)/shard_map/all_to_all | solution.py:49
  138.8 4.0 all-to-all-start.6
  143.7 12.0 %all-to-all-done.6 = f32[128,2,128]{2,1,0:T(2,128)S(1)} async-done(((f32[128,2,128]{2,1,0:T(2,128)}), f32[128,2,128]{2,1,0:T(2,128)S(1)}, u32[]{:S(2)}, u32[]{:S(2)}) %all-to-all-start.6) | async-done | bytes 131104 | tf_op jit(solution)/shard_map/all_to_all | solution.py:45
  161.3 12.2 %all-to-all-done.7 = f32[32,1,256]{2,1,0:T(1,128)S(1)} async-done(((f32[32,1,256]{2,1,0:T(1,128)}), f32[32,1,256]{2,1,0:T(1,128)S(1)}, u32[]{:S(2)}, u32[]{:S(2)}) %all-to-all-start.7) | async-done | bytes 32800 | tf_op jit(solution)/shard_map/all_to_all | solution.py:49
  175.2 8.1 %all-to-all-start.8 = ((bf16[16,128,64]{1,2,0:T(8,128)(2,1)}), bf16[16,128,64]{1,2,0:T(8,128)(2,1)S(1)}, u32[]{:S(2)}, u32[]{:S(2)}) async-start(bf16[16,128,64]{1,2,0:T(8,128)(2,1)} %stack.2), calls=%async_computation.8 | async-start | bytes 524288 | tf_op jit(solution)/shard_map/all_to_all | solution.py:14
  184.7 6.8 %all-to-all-done.8 = bf16[16,128,64]{1,2,0:T(8,128)(2,1)S(1)} async-done(((bf16[16,128,64]{1,2,0:T(8,128)(2,1)}), bf16[16,128,64]{1,2,0:T(8,128)(2,1)S(1)}, u32[]{:S(2)}, u32[]{:S(2)}) %all-to-all-start.8) | async-done | bytes 262176 | tf_op jit(solution)/shard_map/all_to_all | solution.py:14
  193.0 72.6 %reduce-scatter.7.cloned.1.call-done = f32[64,128]{1,0:T(8,128)} async-done(((f32[1024,128]{1,0:T(8,128)}), f32[64,128]{1,0:T(8,128)}) %reduce-scatter.7.cloned.1.call-update) | async-done | bytes 32784
  267.4 22.2 %all_to_all.283 = f32[32,1,256]{2,1,0:T(1,128)S(1)} all-to-all(f32[32,1,256]{2,1,0:T(1,128)S(1)} %reshape.524), channel_id=1, replica_groups=mesh['seq'=32,'chan'=16] {'seq'}, dimensions={0} | all-to-all | bytes 65536 | tf_op jit(solution)/shard_map/all_to_all | solution.py:45
  295.9 13.0 %all-to-all-done.10 = f32[4,64,128]{2,0,1:T(4,128)S(1)} async-done(((f32[4,64,128]{2,0,1:T(4,128)}), f32[4,64,128]{2,0,1:T(4,128)S(1)}, u32[]{:S(2)}, u32[]{:S(2)}) %all-to-all-start.10) | async-done | bytes 131104 | tf_op jit(solution)/shard_map/all_to_all | solution.py:49
  312.5 17.8 %all_to_all.284 = f32[128,2,130]{2,1,0:T(2,128)S(1)} all-to-all(f32[128,2,130]{2,1,0:T(2,128)S(1)} %copy.376), channel_id=1, replica_groups=mesh['seq'=32,'chan'=16] {'seq'}, dimensions={0} | all-to-all | bytes 266240 | tf_op jit(solution)/shard_map/all_to_all | solution.py:45
  331.2 17.5 %all_to_all.285 = f32[4,32,65]{2,0,1:T(4,128)S(1)} all-to-all(f32[4,32,65]{2,0,1:T(4,128)S(1)} %copy.378), channel_id=1, replica_groups=mesh['seq'=32,'chan'=16] {'seq'}, dimensions={1} | all-to-all | bytes 66560 | tf_op jit(solution)/shard_map/all_to_all | solution.py:49
  349.6 15.3 %all_to_all.286 = f32[32,1,256]{2,1,0:T(1,128)S(1)} all-to-all(f32[32,1,256]{2,1,0:T(1,128)S(1)} %reshape.526), channel_id=1, replica_groups=mesh['seq'=32,'chan'=16] {'seq'}, dimensions={0} | all-to-all | bytes 65536 | tf_op jit(solution)/shard_map/all_to_all | solution.py:45
  367.4 4.1 all-to-all-start.14
  371.5 12.8 %all-to-all-done.14 = f32[4,64,128]{2,0,1:T(4,128)S(1)} async-done(((f32[4,64,128]{2,0,1:T(4,128)}), f32[4,64,128]{2,0,1:T(4,128)S(1)}, u32[]{:S(2)}, u32[]{:S(2)}) %all-to-all-start.14) | async-done | bytes 131104 | tf_op jit(solution)/shard_map/all_to_all | solution.py:49
  394.6 11.9 %all-to-all-done.15 = f32[128,2,130]{2,1,0:T(2,128)S(1)} async-done(((f32[128,2,130]{2,1,0:T(2,128)}), f32[128,2,130]{2,1,0:T(2,128)S(1)}, u32[]{:S(2)}, u32[]{:S(2)}) %all-to-all-start.15) | async-done | bytes 133152 | tf_op jit(solution)/shard_map/all_to_all | solution.py:45
  408.0 5.1 all-to-all-start.16
  413.8 11.8 %all-to-all-done.16 = f32[4,32,65]{2,0,1:T(4,128)S(1)} async-done(((f32[4,32,65]{2,0,1:T(4,128)}), f32[4,32,65]{2,0,1:T(4,128)S(1)}, u32[]{:S(2)}, u32[]{:S(2)}) %all-to-all-start.16) | async-done | bytes 33312 | tf_op jit(solution)/shard_map/all_to_all | solution.py:49
  427.0 102.9 %reduce-scatter.5.cloned.1.call-done = f32[32,64]{1,0:T(8,128)} async-done(((f32[1024,64]{1,0:T(8,128)}), f32[32,64]{1,0:T(8,128)}) %reduce-scatter.5.cloned.1.call-update) | async-done | bytes 8208 | tf_op jit(solution)/shard_map/reduce_scatter | solution.py:160
  (210 shorter events, 69.1 us)
Async XLA Ops:
  8.0 183.5 %copy-start = (bf16[1024,64]{0,1:T(8,128)(2,1)S(1)}, bf16[1024,64]{0,1:T(8,128)(2,1)}, u32[]{:S(2)}) copy-start(bf16[1024,64]{0,1:T(8,128)(2,1)} %param.16) | copy-start | bytes 393220
  8.8 0.7 copy-start.5
  8.8 0.7 copy-start.6
  10.2 28.5 %all-to-all-start = ((f32[128,1,66]{2,1,0:T(1,128)}), f32[128,1,66]{2,1,0:T(1,128)S(1)}, u32[]{:S(2)}, u32[]{:S(2)}) async-start(f32[128,1,66]{2,1,0:T(1,128)} %copy.334), calls=%async_computation | async-start | bytes 131072 | tf_op jit(solution)/shard_map/all_to_all | solution.py:45
  40.5 18.4 %all-to-all-start.1 = ((f32[4,64,132]{2,0,1:T(4,128)}), f32[4,64,132]{2,0,1:T(4,128)S(1)}, u32[]{:S(2)}, u32[]{:S(2)}) async-start(f32[4,64,132]{2,0,1:T(4,128)} %copy.336), calls=%async_computation.1 | async-start | bytes 524288 | tf_op jit(solution)/shard_map/all_to_all | solution.py:49
  81.8 3.9 copy-start.2
  81.8 16.4 %all-to-all-start.3 = ((f32[32,1,256]{2,1,0:T(1,128)}), f32[32,1,256]{2,1,0:T(1,128)S(1)}, u32[]{:S(2)}, u32[]{:S(2)}) async-start(f32[32,1,256]{2,1,0:T(1,128)} %reshape.518), calls=%async_computation.3 | async-start | bytes 65536 | tf_op jit(solution)/shard_map/all_to_all | solution.py:49
  118.3 17.0 %all-to-all-start.5 = ((f32[4,64,128]{2,0,1:T(4,128)}), f32[4,64,128]{2,0,1:T(4,128)S(1)}, u32[]{:S(2)}, u32[]{:S(2)}) async-start(f32[4,64,128]{2,0,1:T(4,128)} %copy.349), calls=%async_computation.5 | async-start | bytes 262144 | tf_op jit(solution)/shard_map/all_to_all | solution.py:49
  138.8 16.9 %all-to-all-start.6 = ((f32[128,2,128]{2,1,0:T(2,128)}), f32[128,2,128]{2,1,0:T(2,128)S(1)}, u32[]{:S(2)}, u32[]{:S(2)}) async-start(f32[128,2,128]{2,1,0:T(2,128)} %copy.359), calls=%async_computation.6 | async-start | bytes 262144 | tf_op jit(solution)/shard_map/all_to_all | solution.py:45
  142.8 0.7 copy-start.8
  157.2 3.9 copy-start.7
  157.2 4.0 copy-start.3
  157.2 16.3 %all-to-all-start.7 = ((f32[32,1,256]{2,1,0:T(1,128)}), f32[32,1,256]{2,1,0:T(1,128)S(1)}, u32[]{:S(2)}, u32[]{:S(2)}) async-start(f32[32,1,256]{2,1,0:T(1,128)} %reshape.522), calls=%async_computation.7 | async-start | bytes 65536 | tf_op jit(solution)/shard_map/all_to_all | solution.py:49
  175.2 8.2 %copy-start.1 = (f32[25426]{0:T(1024)S(1)}, f32[25426]{0:T(1024)}, u32[]{:S(2)}) copy-start(f32[25426]{0:T(1024)} %param.19) | copy-start | bytes 305116
  175.2 16.3 %all-to-all-start.8 = ((bf16[16,128,64]{1,2,0:T(8,128)(2,1)}), bf16[16,128,64]{1,2,0:T(8,128)(2,1)S(1)}, u32[]{:S(2)}, u32[]{:S(2)}) async-start(bf16[16,128,64]{1,2,0:T(8,128)(2,1)} %stack.2), calls=%async_computation.8 | async-start | bytes 524288 | tf_op jit(solution)/shard_map/all_to_all | solution.py:14
  183.3 82.3 %reduce-scatter.7.cloned.1.call-start = ((), (), s32[]{:S(2)}) async-start(), calls=%async_computation.20 | async-start | bytes 557056
  183.4 8.1 %copy-start.4 = (bf16[128,64]{0,1:T(8,128)(2,1)S(1)}, bf16[128,64]{0,1:T(8,128)(2,1)}, u32[]{:S(2)}) copy-start(bf16[128,64]{0,1:T(8,128)(2,1)} %param.15) | copy-start | bytes 49156
  292.1 16.9 %all-to-all-start.10 = ((f32[4,64,128]{2,0,1:T(4,128)}), f32[4,64,128]{2,0,1:T(4,128)S(1)}, u32[]{:S(2)}, u32[]{:S(2)}) async-start(f32[4,64,128]{2,0,1:T(4,128)} %copy.366), calls=%async_computation.10 | async-start | bytes 262144 | tf_op jit(solution)/shard_map/all_to_all | solution.py:49
  367.4 16.9 %all-to-all-start.14 = ((f32[4,64,128]{2,0,1:T(4,128)}), f32[4,64,128]{2,0,1:T(4,128)S(1)}, u32[]{:S(2)}, u32[]{:S(2)}) async-start(f32[4,64,128]{2,0,1:T(4,128)} %copy.381), calls=%async_computation.14 | async-start | bytes 262144 | tf_op jit(solution)/shard_map/all_to_all | solution.py:49
  388.2 18.3 %all-to-all-start.15 = ((f32[128,2,130]{2,1,0:T(2,128)}), f32[128,2,130]{2,1,0:T(2,128)S(1)}, u32[]{:S(2)}, u32[]{:S(2)}) async-start(f32[128,2,130]{2,1,0:T(2,128)} %copy.387), calls=%async_computation.15 | async-start | bytes 524288 | tf_op jit(solution)/shard_map/all_to_all | solution.py:45
  392.1 137.8 %reduce-scatter.5.cloned.1.call-start = ((), (), s32[]{:S(2)}) async-start(), calls=%async_computation.19 | async-start | bytes 540672 | tf_op jit(solution)/shard_map/reduce_scatter | solution.py:160
  408.0 17.6 %all-to-all-start.16 = ((f32[4,32,65]{2,0,1:T(4,128)}), f32[4,32,65]{2,0,1:T(4,128)S(1)}, u32[]{:S(2)}, u32[]{:S(2)}) async-start(f32[4,32,65]{2,0,1:T(4,128)} %copy.389), calls=%async_computation.16 | async-start | bytes 131072 | tf_op jit(solution)/shard_map/all_to_all | solution.py:49
Sparse Core Ops, SparseCore 0:
  193.1 72.4 reduce-scatter.6
Sparse Core Ops, SparseCore 1:
  398.4 131.4 reduce-scatter.4
